TPU v7x, 256 devices: a whole 4x4x8 slice. The times are simulated.
256 devices in a mesh: pb: 8 (over x, y_lo), ka: 4 (over y_hi, core), ha: 8 (over z).
Axes of the slice: x: 4, y: 4 (y_hi: 2, y_lo: 2; y = y_hi * 2 + y_lo), z: 8, core: 2. Of those that a mesh axis runs over, the one named last changes fastest.
Arguments:
- queries: bfloat16 [4096, 64, 128], P(('pb', 'ka'), 'ha'), may hold values from -8 to 8
- keys: bfloat16 [4096, 8, 128], P(('pb', 'ka'), 'ha'), may hold values from -4.5 to 4.5
- values: bfloat16 [4096, 8, 128], P(('pb', 'ka'), 'ha'), may hold values from -12 to 12
- out_grad: bfloat16 [4096, 64, 128], P(('pb', 'ka'), 'ha'), may hold values from -6 to 6
Outputs:
- attended: bfloat16 [4096, 64, 128], P(('pb', 'ka'), 'ha')
- query_grad: bfloat16 [4096, 64, 128], P(('pb', 'ka'), 'ha')
- key_grad: bfloat16 [4096, 8, 128], P(('pb', 'ka'), 'ha')
- value_grad: bfloat16 [4096, 8, 128], P(('pb', 'ka'), 'ha')
All inputs are finite; a program needn't handle non-finite values.
Results may differ from a plain program's by a relative error of at most 0.0097.
Values may be sent and summed in bfloat16 or wider, within the bound.
No kernel may reach another device: no remote copies, remote signals or barrier semaphores. Data moves between devices by JAX's collectives and lax.ppermute only.
A program may use at most 128 MiB of HBM per device.

v0:
```python
import math
import jax
import jax.numpy as jnp
from jax import lax
from jax.sharding import PartitionSpec as P

HEAD_DIM = 128
GROUP = 8


def merged(value, axis, join):
    pieces = jax.tree.map(lambda part: lax.all_gather(part, axis), value)
    head = jax.tree.map(lambda part: part[0], pieces)
    tail = jax.tree.map(lambda part: part[1:], pieces)
    total, _ = lax.scan(lambda total, section: (join(total, section), None), head, tail)
    return total


def combine_partials(earlier, second):
    earlier_max, earlier_total, earlier_sum = earlier
    second_max, second_total, second_sum = second
    joined = jnp.maximum(earlier_max, second_max)
    earlier_factor = jnp.exp(earlier_max - joined)
    second_factor = jnp.exp(second_max - joined)
    merged_total = earlier_total * earlier_factor + second_total * second_factor
    merged_sum = earlier_sum * earlier_factor[..., None] + second_sum * second_factor[..., None]
    return (joined, merged_total, merged_sum)


def make_absorb(grouped, scaling, running, pieces):
    run_max, run_total, run_sum = running
    key_piece, value_piece = pieces
    scores = (
        jnp.einsum("qhgd,khd->hgqk", grouped, key_piece, preferred_element_type=jnp.float32)
        * scaling
    )
    new_max = jnp.max(scores, axis=-1)
    factor = jnp.exp(run_max - new_max)
    weights = jnp.exp(scores - new_max[..., None])
    run_total = run_total * factor + jnp.sum(weights, axis=-1)
    run_sum = run_sum * factor[..., None] + jnp.einsum(
        "hgqk,khd->hgqd",
        weights,
        value_piece.astype(jnp.float32),
        preferred_element_type=jnp.float32,
        precision=lax.Precision.HIGHEST,
    )
    return (new_max, run_total, run_sum)


def start_stats(kv_count, query_total):
    stat_shape = (kv_count, GROUP, query_total)
    return (
        jnp.full(stat_shape, -jnp.inf, jnp.float32),
        jnp.zeros(stat_shape, jnp.float32),
        jnp.zeros(stat_shape + (HEAD_DIM,), jnp.float32),
    )


def backward_blocks(query_heads, grad_heads, log_total, row_dots, key_rows, value_rows, scaling):
    key_total = key_rows.shape[0]
    block_width = math.gcd(key_total, 512)

    def visit_block(grad_running, position):
        first_row = position * block_width
        key_block = lax.dynamic_slice_in_dim(key_rows, first_row, block_width, 0)
        value_block = lax.dynamic_slice_in_dim(value_rows, first_row, block_width, 0)
        scores = (
            jnp.einsum("qhgd,khd->hgqk", query_heads, key_block, preferred_element_type=jnp.float32)
            * scaling
        )
        probs = jnp.exp(scores - log_total[..., None])
        value_part = jnp.einsum(
            "hgqk,qhgd->khd",
            probs.astype(jnp.bfloat16),
            grad_heads,
            preferred_element_type=jnp.float32,
        )
        grad_probs = jnp.einsum(
            "qhgd,khd->hgqk", grad_heads, value_block, preferred_element_type=jnp.float32
        )
        grad_scores = (scaling * probs * (grad_probs - row_dots[..., None])).astype(jnp.bfloat16)
        grad_running = grad_running + jnp.einsum(
            "hgqk,khd->qhgd", grad_scores, key_block, preferred_element_type=jnp.float32
        )
        key_part = jnp.einsum(
            "hgqk,qhgd->khd", grad_scores, query_heads, preferred_element_type=jnp.float32
        )
        return (grad_running, (key_part, value_part))

    initial = jnp.zeros(query_heads.shape, jnp.float32)
    block_count = key_total // block_width
    grad_query, (key_parts, value_parts) = lax.scan(
        visit_block, initial, jnp.arange(block_count, dtype=jnp.int32)
    )
    tail_shape = key_rows.shape
    return (grad_query, key_parts.reshape(tail_shape), value_parts.reshape(tail_shape))


def on_device(queries, keys, values, out_grad):
    local_rows = queries.shape[0]
    head_count = queries.shape[1]
    kv_count = keys.shape[1]
    scaling = HEAD_DIM ** (-0.5)
    own_queries = queries.reshape(local_rows, kv_count, GROUP, HEAD_DIM)
    block_queries = lax.all_gather(queries, "ka", axis=0, tiled=True)
    query_total = block_queries.shape[0]
    grouped = block_queries.reshape(query_total, kv_count, GROUP, HEAD_DIM)
    local_parts = make_absorb(
        grouped,
        scaling,
        start_stats(kv_count, query_total),
        (
            lax.all_gather(keys, "pb", axis=0, tiled=True),
            lax.all_gather(values, "pb", axis=0, tiled=True),
        ),
    )
    whole_max, whole_total, whole_sum = merged(local_parts, "ka", combine_partials)
    first_row = lax.axis_index("ka") * local_rows
    own_max = lax.dynamic_slice_in_dim(whole_max, first_row, local_rows, 2)
    own_total = lax.dynamic_slice_in_dim(whole_total, first_row, local_rows, 2)
    own_sum = lax.dynamic_slice_in_dim(whole_sum, first_row, local_rows, 2)
    exact_out = own_sum / own_total[..., None]
    output_heads = exact_out.astype(jnp.bfloat16)
    log_total = own_max + jnp.log(own_total)
    attended = jnp.transpose(output_heads, (2, 0, 1, 3)).reshape(local_rows, head_count, HEAD_DIM)
    grad_heads = out_grad.reshape(local_rows, kv_count, GROUP, HEAD_DIM)
    row_dots = jnp.einsum(
        "hgqd,qhgd->hgq",
        exact_out,
        grad_heads.astype(jnp.float32),
        preferred_element_type=jnp.float32,
    )
    wide_key, wide_value = (
        lax.all_gather(keys, ("pb", "ka"), axis=0, tiled=True),
        lax.all_gather(values, ("pb", "ka"), axis=0, tiled=True),
    )
    grad_query, key_terms, value_terms = backward_blocks(
        own_queries, grad_heads, log_total, row_dots, wide_key, wide_value, scaling
    )
    grad_key, grad_value = (
        lax.psum_scatter(key_terms, ("pb", "ka"), scatter_dimension=0, tiled=True),
        lax.psum_scatter(value_terms, ("pb", "ka"), scatter_dimension=0, tiled=True),
    )
    query_grad = grad_query.astype(jnp.bfloat16).reshape(local_rows, head_count, HEAD_DIM)
    return (attended, query_grad, grad_key.astype(jnp.bfloat16), grad_value.astype(jnp.bfloat16))


def solution(mesh):
    return jax.shard_map(
        on_device,
        mesh=mesh,
        in_specs=(
            P(("pb", "ka"), "ha", None),
            P(("pb", "ka"), "ha", None),
            P(("pb", "ka"), "ha", None),
            P(("pb", "ka"), "ha", None),
        ),
        out_specs=(
            P(("pb", "ka"), "ha", None),
            P(("pb", "ka"), "ha", None),
            P(("pb", "ka"), "ha", None),
            P(("pb", "ka"), "ha", None),
        ),
        check_vma=False,
    )
```

profile of v0, /device:TPU:32, one launch (start us, length us, event | category | flops | bytes accessed | tf_op | source)
XLA Modules:
  0.0 639.3 jit_solution(16966723260642444875)
XLA Ops:
  7.2 1.7 copy.52
  9.0 28.9 %all_gather.31 = bf16[1024,1,128]{2,0,1:T(8,128)(2,1)S(1)} all-gather(bf16[128,1,128]{2,0,1:T(8,128)(2,1)} %param.9), channel_id=1, replica_groups=mesh['pb'=8,'ka'=4,'ha'=8] {'pb'}, dimensions={0}, use_global_device_ids=true | all-gather | bytes 294912 | tf_op jit(solution)/shard_map/all_gather | solution.py:114
  37.9 28.7 %all_gather.36 = bf16[1024,1,128]{2,0,1:T(8,128)(2,1)S(1)} all-gather(bf16[128,1,128]{2,0,1:T(8,128)(2,1)} %param.10), channel_id=1, replica_groups=mesh['pb'=8,'ka'=4,'ha'=8] {'pb'}, dimensions={0}, use_global_device_ids=true | all-gather | bytes 294912 | tf_op jit(solution)/shard_map/all_gather | solution.py:115
  66.6 9.3 %bitcast_reduce_fusion = (f32[8,512]{1,0:T(8,128)S(1)}, f32[1024,512,8]{1,0,2:T(8,128)}) fusion(bf16[512,8,128]{2,0,1:T(8,128)(2,1)} %all-gather.7.cloned.1.call-done, bf16[1024,1,128]{2,0,1:T(8,128)(2,1)S(1)} %all_gather.31), kind=kOutput, calls=%fused_computation.44 | convolution fusion | flops 1082126336 | bytes 18104320 | tf_op jit(solution)/shard_map/qhgd,khd->hgqk/dot_general | solution.py:34
  75.9 8.5 %fusion.36 = f32[8,512]{1,0:T(8,128)S(1)} fusion(f32[1024,512,8]{1,0,2:T(8,128)} %get-tuple-element.212, f32[8,512]{1,0:T(8,128)S(1)} %get-tuple-element.211), kind=kLoop, calls=%fused_computation.46 | loop fusion | flops 12578816 | bytes 16809984 | tf_op jit(solution)/shard_map/reduce_sum | solution.py:40
  84.4 18.9 %fusion.39 = f32[8,512,128]{2,1,0:T(8,128)} fusion(f32[1024,512,8]{1,0,2:T(8,128)} %get-tuple-element.212, f32[8,512]{1,0:T(8,128)S(1)} %get-tuple-element.211, f32[8,512]{1,0:T(8,128)S(1)} %get-tuple-element.209, bf16[1024,1,128]{2,0,1:T(8,128)(2,1)S(1)} %all_gather.36), kind=kOutput, calls=%fused_computation.50 | convolution fusion | flops 6451363840 | bytes 19169280 | tf_op jit(solution)/shard_map/hgqk,khd->hgqd/dot_general | solution.py:41
  104.8 6.7 %all_gather.35 = f32[4,1,8,512]{3,2,1,0:T(8,128)S(1)} all-gather(f32[1,1,8,512]{3,2,1,0:T(8,128)S(1)} %get-tuple-element.210), channel_id=1, replica_groups=mesh['pb'=8,'ka'=4,'ha'=8] {'ka'}, dimensions={0}, use_global_device_ids=true | all-gather | bytes 81920 | tf_op jit(solution)/shard_map/all_gather | solution.py:12
  111.5 6.8 %all-gather = f32[32,512]{1,0:T(8,128)S(1)} all-gather(f32[8,512]{1,0:T(8,128)S(1)} %get-tuple-element.211), channel_id=2, replica_groups=mesh['pb'=8,'ka'=4,'ha'=8] {'ka'}, dimensions={0}, use_global_device_ids=true | all-gather | bytes 81920 | tf_op jit(solution)/shard_map/all_gather | solution.py:12
  118.3 52.3 %all-gather.13.cloned.1.call-done = f32[32,512,128]{2,1,0:T(8,128)} async-done(((f32[8,512,128]{2,1,0:T(8,128)}), f32[32,512,128]{2,1,0:T(8,128)}) %all-gather.13.cloned.1.call-update) | async-done | bytes 8388624 | tf_op jit(solution)/shard_map/all_gather | solution.py:12
  170.6 6.1 slice.33
  176.7 1.7 slice_bitcast_fusion
  178.4 8.6 %while.29 = (s32[]{:T(128)}, f32[1,8,512]{2,1,0:T(8,128)S(1)}, f32[1,8,512]{2,1,0:T(8,128)S(1)}, f32[1,8,512,128]{3,2,1,0:T(8,128)S(1)}, f32[3,1,8,512]{3,2,1,0:...) while((s32[]{:T(128)}, f32[1,8,512]{2,1,0:T(8,128)S(1)}, ...), condition=%wide.region_3.4_spmd, body=%wide.region_2.3_spmd.sunk | while | flops 1601538 | bytes 6537313 | solution.py:15
  178.7 2.7 fusion.70
  181.5 2.7 fusion.70
  184.3 2.7 fusion.70
  187.0 2.5 copy.33
  189.7 1.4 fusion.42
  191.2 38.9 %all-gather.11.cloned.1.call-done = bf16[4096,1,128]{2,0,1:T(8,128)(2,1)} async-done(((bf16[128,1,128]{2,0,1:T(8,128)(2,1)}), bf16[4096,1,128]{2,0,1:T(8,128)(2,1)}) %all-gather.11.cloned.1.call-update) | async-done | bytes 1048592 | tf_op jit(solution)/shard_map/all_gather | solution.py:136
  230.1 59.3 %all-gather.9.cloned.1.call-done = bf16[4096,1,128]{2,0,1:T(8,128)(2,1)} async-done(((bf16[128,1,128]{2,0,1:T(8,128)(2,1)}), bf16[4096,1,128]{2,0,1:T(8,128)(2,1)}) %all-gather.9.cloned.1.call-update) | async-done | bytes 1048592 | tf_op jit(solution)/shard_map/all_gather | solution.py:135
  289.5 63.0 %while.30 = (s32[]{:T(128)}, f32[128,1,8,128]{0,3,2,1:T(8,128)S(1)}, f32[8,512,1,128]{3,1,2,0:T(8,128)}, f32[8,512,1,128]{3,1,2,0:T(8,128)}, s32[8]{0:T(128)S(1)...) while((s32[]{:T(128)}, ...), condition=%wide.region_5.6_spmd.clone, body=%wide.region_4.5_spmd.clone.sunk | while | flops 676069376 | bytes 12465373 | solution.py:93
  290.7 1.3 fusion.81
  292.0 1.6 fusion.82
  293.7 1.2 fusion.84
  294.8 1.2 fusion.85
  296.0 1.3 fusion.83
  298.6 1.3 fusion.81
  299.9 1.6 fusion.82
  302.7 1.2 fusion.85
  303.9 1.3 fusion.83
  306.4 1.3 fusion.81
  307.8 1.6 fusion.82
  309.4 1.2 fusion.84
  310.6 1.2 fusion.85
  311.7 1.3 fusion.83
  314.3 1.3 fusion.81
  315.7 1.6 fusion.82
  317.3 1.2 fusion.84
  318.4 1.2 fusion.85
  319.6 1.3 fusion.83
  322.2 1.3 fusion.81
  323.5 1.6 fusion.82
  325.2 1.2 fusion.84
  326.3 1.2 fusion.85
  327.5 1.3 fusion.83
  330.1 1.3 fusion.81
  331.4 1.6 fusion.82
  333.0 1.2 fusion.84
  334.2 1.2 fusion.85
  335.4 1.3 fusion.83
  338.0 1.3 fusion.81
  339.3 1.6 fusion.82
  340.9 1.2 fusion.84
  342.1 1.2 fusion.85
  343.3 1.3 fusion.83
  345.9 1.3 fusion.81
  347.2 1.6 fusion.82
  348.8 1.2 fusion.84
  350.0 1.2 fusion.85
  351.2 1.3 fusion.83
  354.0 2.0 convert_bitcast_fusion.1
  356.0 136.3 %reduce-scatter.3.cloned.1.call-done = f32[128,1,128]{2,0,1:T(8,128)} async-done(((f32[4096,1,128]{2,0,1:T(8,128)}), f32[128,1,128]{2,0,1:T(8,128)}) %reduce-scatter.3.cloned.1.call-update) | async-done | bytes 65552 | tf_op jit(solution)/shard_map/reduce_scatter | solution.py:142
  492.3 1.5 convert_element_type.22
  493.7 137.3 %reduce-scatter.5.cloned.1.call-done = f32[128,1,128]{2,0,1:T(8,128)} async-done(((f32[4096,1,128]{2,0,1:T(8,128)}), f32[128,1,128]{2,0,1:T(8,128)}) %reduce-scatter.5.cloned.1.call-update) | async-done | bytes 65552 | tf_op jit(solution)/shard_map/reduce_scatter | solution.py:143
  631.0 1.5 convert_element_type.23
  (49 shorter events, 9.1 us)
Async XLA Ops:
  7.2 59.4 %all-gather.7.cloned.1.call-start = ((), (), s32[]{:S(2)}) async-start(), calls=%async_computation.2 | async-start | bytes 1310720 | tf_op jit(solution)/shard_map/all_gather | solution.py:106
  8.9 161.7 %all-gather.13.cloned.1.call-start = ((), (), s32[]{:S(2)}) async-start(), calls=%async_computation.7 | async-start | bytes 10485760 | tf_op jit(solution)/shard_map/all_gather | solution.py:12
  103.3 1.4 copy-start.1
  103.3 126.8 %all-gather.11.cloned.1.call-start = ((), (), s32[]{:S(2)}) async-start(), calls=%async_computation.4 | async-start | bytes 1081344 | tf_op jit(solution)/shard_map/all_gather | solution.py:136
  104.1 185.4 %all-gather.9.cloned.1.call-start = ((), (), s32[]{:S(2)}) async-start(), calls=%async_computation.3 | async-start | bytes 1081344 | tf_op jit(solution)/shard_map/all_gather | solution.py:135
  104.7 387.6 %reduce-scatter.3.cloned.1.call-start = ((), (), s32[]{:S(2)}) async-start(), calls=%async_computation.5 | async-start | bytes 2162688 | tf_op jit(solution)/shard_map/reduce_scatter | solution.py:142
  187.0 102.4 %copy-start = (bf16[128,8,128]{2,0,1:T(8,128)(2,1)S(1)}, bf16[128,8,128]{2,0,1:T(8,128)(2,1)}, u32[]{:S(2)}) copy-start(bf16[128,8,128]{2,0,1:T(8,128)(2,1)} %copy.52) | copy-start | bytes 786436
  352.5 278.5 %reduce-scatter.5.cloned.1.call-start = ((), (), s32[]{:S(2)}) async-start(), calls=%async_computation.6 | async-start | bytes 2162688 | tf_op jit(solution)/shard_map/reduce_scatter | solution.py:143
Sparse Core Ops, SparseCore 0:
  10.4 27.1 all-gather.6
  103.5 67.0 all-gather.12
  172.5 57.5 all-gather.10
  231.8 57.5 all-gather.8
  352.6 139.5 reduce-scatter.2
  494.6 136.3 reduce-scatter.4
where the time goes:
time: 640 us; the launch traced here: 639 us
  waiting for transfers between devices  426 us (67%)
  matrix products  81 us (13%)
  blocking collectives  71.1 us (11%)
  other arithmetic  23 us (4%)
  local copies, waits for them, and re-layouts  17.9 us (3%)
  between operations  14.2 us (2%)
    reduce_scatter x1, waiting for transfers between devices, on_device(): lax.psum_scatter(value_terms, ('pb', 'ka'), scatter_dimension=0, tiled=True)  137 us
    reduce_scatter x1, waiting for transfers between devices, on_device(): lax.psum_scatter(key_terms, ('pb', 'ka'), scatter_dimension=0, tiled=True)  136 us
    all_gather x1, waiting for transfers between devices, on_device(): lax.all_gather(keys, ('pb', 'ka'), axis=0, tiled=True)  59.3 us
    all_gather x1, waiting for transfers between devices, merged(): pieces = jax.tree.map(lambda part: lax.all_gather(part, axis), value)  52.3 us
    all_gather x1, waiting for transfers between devices, on_device(): lax.all_gather(values, ('pb', 'ka'), axis=0, tiled=True)  38.9 us
    all_gather x1, blocking collectives, on_device(): lax.all_gather(keys, 'pb', axis=0, tiled=True)  28.9 us
    all_gather x1, blocking collectives, on_device(): lax.all_gather(values, 'pb', axis=0, tiled=True)  28.7 us
    dot_general x1, matrix products, make_absorb(): jnp.einsum('hgqk,khd->hgqd', weights, value_piece.astype(jnp.float32), pr...  18.9 us
  transfers between devices with their start and end apart: 6, of which 5 were waited for; matrix products, arithmetic and copies ran while one was open for 4% of the time, Pallas kernels for 0%

commit v1 on v0

--- a/solution.py
+++ b/solution.py
@@ -132,7 +132,10 @@
         preferred_element_type=jnp.float32,
     )
     wide_key, wide_value = (
-        lax.all_gather(keys, ("pb", "ka"), axis=0, tiled=True),
+        jnp.concatenate(
+            lax.all_to_all(jnp.stack([keys] * lax.axis_size(("pb", "ka"))), ("pb", "ka"), 0, 0),
+            axis=0,
+        ),
         lax.all_gather(values, ("pb", "ka"), axis=0, tiled=True),
     )
     grad_query, key_terms, value_terms = backward_blocks(

time: 640 us -> 586 us (0.916)
  waiting for transfers between devices: 426 us -> 353 us
  blocking collectives: 71.1 us -> 81.6 us
  starting transfers between devices: 0.24 us -> 6.96 us
    all_gather x1 -> x0, waiting for transfers between devices: 59.3 us -> none  [on_device(): lax.all_gather(keys, ('pb', 'ka'), axis=0, tiled=True)]
    all_gather x1, waiting for transfers between devices: 52.3 us -> 38.8 us  [merged(): pieces = jax.tree.map(lambda part: lax.all_gather(part, axis), value)]
    all_gather x2, blocking collectives: 13.5 us -> 24 us  [merged(): pieces = jax.tree.map(lambda part: lax.all_gather(part, axis), value)]
    all_to_all x0 -> x1, starting transfers between devices: none -> 6.76 us  [on_device(): lax.all_to_all(jnp.stack([keys] * lax.axis_size(('pb', 'ka'))), ('pb', 'k...]
  transfers between devices with their start and end apart: 6 -> 6, of which waited for: 5 -> 4; matrix products, arithmetic and copies ran while one was open for 4% -> 4% of each run, Pallas kernels for 0% -> 0%
where the time goes in v1:
time: 586 us; the launch traced here: 585 us
  waiting for transfers between devices  353 us (60%)
  blocking collectives  81.6 us (14%)
  matrix products  81 us (14%)
  other arithmetic  23 us (4%)
  local copies, waits for them, and re-layouts  19.8 us (3%)
  between operations  13.9 us (2%)
  starting transfers between devices  6.96 us (1%)
  loops' own time  5.88 us (1%)
    reduce_scatter x1, waiting for transfers between devices, on_device(): lax.psum_scatter(value_terms, ('pb', 'ka'), scatter_dimension=0, tiled=True)  137 us
    reduce_scatter x1, waiting for transfers between devices, on_device(): lax.psum_scatter(key_terms, ('pb', 'ka'), scatter_dimension=0, tiled=True)  136 us
    all_gather x1, waiting for transfers between devices, on_device(): lax.all_gather(values, ('pb', 'ka'), axis=0, tiled=True)  39.9 us
    all_gather x1, waiting for transfers between devices, merged(): pieces = jax.tree.map(lambda part: lax.all_gather(part, axis), value)  38.8 us
    all_gather x1, blocking collectives, on_device(): lax.all_gather(keys, 'pb', axis=0, tiled=True)  28.9 us
    all_gather x1, blocking collectives, on_device(): lax.all_gather(values, 'pb', axis=0, tiled=True)  28.7 us
    all_gather x2, blocking collectives, merged(): pieces = jax.tree.map(lambda part: lax.all_gather(part, axis), value)  24 us
    dot_general x1, matrix products, make_absorb(): jnp.einsum('hgqk,khd->hgqd', weights, value_piece.astype(jnp.float32), pr...  18.9 us
  transfers between devices with their start and end apart: 6, of which 4 were waited for; matrix products, arithmetic and copies ran while one was open for 4% of the time, Pallas kernels for 0%

profile of v1, /device:TPU:32, one launch (start us, length us, event | category | flops | bytes accessed | tf_op | source)
XLA Modules:
  0.0 585.1 jit_solution(3431825439154348425)
XLA Ops:
  7.2 1.7 copy.52
  9.0 28.9 %all_gather.28 = bf16[1024,1,128]{2,0,1:T(8,128)(2,1)S(1)} all-gather(bf16[128,1,128]{2,0,1:T(8,128)(2,1)} %param.9), channel_id=1, replica_groups=mesh['pb'=8,'ka'=4,'ha'=8] {'pb'}, dimensions={0}, use_global_device_ids=true | all-gather | bytes 294912 | tf_op jit(solution)/shard_map/all_gather | solution.py:114
  37.9 28.7 %all_gather.33 = bf16[1024,1,128]{2,0,1:T(8,128)(2,1)S(1)} all-gather(bf16[128,1,128]{2,0,1:T(8,128)(2,1)} %param.10), channel_id=1, replica_groups=mesh['pb'=8,'ka'=4,'ha'=8] {'pb'}, dimensions={0}, use_global_device_ids=true | all-gather | bytes 294912 | tf_op jit(solution)/shard_map/all_gather | solution.py:115
  66.6 9.3 %bitcast_reduce_fusion = (f32[8,512]{1,0:T(8,128)S(1)}, f32[1024,512,8]{1,0,2:T(8,128)}) fusion(bf16[512,8,128]{2,0,1:T(8,128)(2,1)} %all-gather.6.cloned.1.call-done, bf16[1024,1,128]{2,0,1:T(8,128)(2,1)S(1)} %all_gather.28), kind=kOutput, calls=%fused_computation.44 | convolution fusion | flops 1082126336 | bytes 18104320 | tf_op jit(solution)/shard_map/qhgd,khd->hgqk/dot_general | solution.py:34
  75.9 8.5 %fusion.36 = f32[8,512]{1,0:T(8,128)S(1)} fusion(f32[1024,512,8]{1,0,2:T(8,128)} %get-tuple-element.212, f32[8,512]{1,0:T(8,128)S(1)} %get-tuple-element.211), kind=kLoop, calls=%fused_computation.46 | loop fusion | flops 12578816 | bytes 16809984 | tf_op jit(solution)/shard_map/reduce_sum | solution.py:40
  84.4 18.9 %fusion.39 = f32[8,512,128]{2,1,0:T(8,128)} fusion(f32[1024,512,8]{1,0,2:T(8,128)} %get-tuple-element.212, f32[8,512]{1,0:T(8,128)S(1)} %get-tuple-element.211, f32[8,512]{1,0:T(8,128)S(1)} %get-tuple-element.209, bf16[1024,1,128]{2,0,1:T(8,128)(2,1)S(1)} %all_gather.33), kind=kOutput, calls=%fused_computation.50 | convolution fusion | flops 6451363840 | bytes 19169280 | tf_op jit(solution)/shard_map/hgqk,khd->hgqd/dot_general | solution.py:41
  104.1 1.2 stack.2
  105.3 6.8 %all-to-all-start = ((bf16[32,128,1,128]{3,1,2,0:T(8,128)(2,1)}), bf16[32,128,1,128]{3,1,2,0:T(8,128)(2,1)}, u32[]{:S(2)}, u32[]{:S(2)}) async-start(bf16[32,128,1,128]{3,1,2,0:T(8,128)(2,1)} %stack.2), calls=%async_computation | async-start | bytes 2097152 | tf_op jit(solution)/shard_map/all_to_all | solution.py:136
  112.9 16.8 %all_gather.32 = f32[4,1,8,512]{3,2,1,0:T(8,128)S(1)} all-gather(f32[1,1,8,512]{3,2,1,0:T(8,128)S(1)} %get-tuple-element.210), channel_id=1, replica_groups=mesh['pb'=8,'ka'=4,'ha'=8] {'ka'}, dimensions={0}, use_global_device_ids=true | all-gather | bytes 81920 | tf_op jit(solution)/shard_map/all_gather | solution.py:12
  129.8 7.1 %all-gather = f32[32,512]{1,0:T(8,128)S(1)} all-gather(f32[8,512]{1,0:T(8,128)S(1)} %get-tuple-element.211), channel_id=2, replica_groups=mesh['pb'=8,'ka'=4,'ha'=8] {'ka'}, dimensions={0}, use_global_device_ids=true | all-gather | bytes 81920 | tf_op jit(solution)/shard_map/all_gather | solution.py:12
  136.9 38.8 %all-gather.10.cloned.1.call-done = f32[32,512,128]{2,1,0:T(8,128)} async-done(((f32[8,512,128]{2,1,0:T(8,128)}), f32[32,512,128]{2,1,0:T(8,128)}) %all-gather.10.cloned.1.call-update) | async-done | bytes 8388624 | tf_op jit(solution)/shard_map/all_gather | solution.py:12
  175.7 6.1 %slice.33 = f32[24,512,128]{2,1,0:T(8,128)} slice(f32[32,512,128]{2,1,0:T(8,128)} %all-gather.10.cloned.1.call-done), slice={[8:32], [0:512], [0:128]} | slice | bytes 12582912 | tf_op jit(solution)/shard_map/slice | solution.py:14
  181.8 1.7 slice_bitcast_fusion
  183.5 8.6 %while.29 = (s32[]{:T(128)}, f32[1,8,512]{2,1,0:T(8,128)S(1)}, f32[1,8,512]{2,1,0:T(8,128)S(1)}, f32[1,8,512,128]{3,2,1,0:T(8,128)S(1)}, f32[3,1,8,512]{3,2,1,0:...) while((s32[]{:T(128)}, f32[1,8,512]{2,1,0:T(8,128)S(1)}, ...), condition=%wide.region_3.4_spmd, body=%wide.region_2.3_spmd.sunk | while | flops 1601538 | bytes 6537313 | solution.py:15
  183.8 2.7 fusion.70
  186.6 2.7 fusion.70
  189.4 2.7 fusion.70
  192.1 2.5 copy.33
  194.8 1.4 fusion.42
  196.2 39.9 %all-gather.8.cloned.1.call-done = bf16[4096,1,128]{2,0,1:T(8,128)(2,1)} async-done(((bf16[128,1,128]{2,0,1:T(8,128)(2,1)}), bf16[4096,1,128]{2,0,1:T(8,128)(2,1)}) %all-gather.8.cloned.1.call-update) | async-done | bytes 1048592 | tf_op jit(solution)/shard_map/all_gather | solution.py:139
  236.1 63.0 %while.30 = (s32[]{:T(128)}, f32[128,1,8,128]{0,3,2,1:T(8,128)S(1)}, f32[8,512,1,128]{3,1,2,0:T(8,128)}, f32[8,512,1,128]{3,1,2,0:T(8,128)}, s32[8]{0:T(128)S(1)...) while((s32[]{:T(128)}, ...), condition=%wide.region_5.6_spmd.clone, body=%wide.region_4.5_spmd.clone.sunk | while | flops 676069376 | bytes 12465373 | solution.py:93
  237.4 1.3 fusion.81
  238.7 1.6 fusion.82
  240.3 1.2 fusion.84
  241.5 1.2 fusion.85
  242.7 1.3 fusion.83
  245.3 1.3 fusion.81
  246.6 1.6 fusion.82
  249.4 1.2 fusion.85
  250.6 1.3 fusion.83
  253.1 1.3 fusion.81
  254.5 1.6 fusion.82
  256.1 1.2 fusion.84
  257.3 1.2 fusion.85
  258.4 1.3 fusion.83
  261.0 1.3 fusion.81
  262.3 1.6 fusion.82
  264.0 1.2 fusion.84
  265.1 1.2 fusion.85
  266.3 1.3 fusion.83
  268.9 1.3 fusion.81
  270.2 1.6 fusion.82
  273.0 1.2 fusion.85
  274.2 1.3 fusion.83
  276.8 1.3 fusion.81
  278.1 1.6 fusion.82
  279.7 1.2 fusion.84
  280.9 1.2 fusion.85
  282.1 1.3 fusion.83
  284.7 1.3 fusion.81
  286.0 1.6 fusion.82
  287.6 1.2 fusion.84
  288.8 1.2 fusion.85
  290.0 1.3 fusion.83
  292.5 1.3 fusion.81
  293.9 1.6 fusion.82
  295.5 1.2 fusion.84
  296.7 1.2 fusion.85
  297.9 1.3 fusion.83
  300.7 2.0 convert_bitcast_fusion.1
  302.7 135.9 %reduce-scatter.3.cloned.1.call-done = f32[128,1,128]{2,0,1:T(8,128)} async-done(((f32[4096,1,128]{2,0,1:T(8,128)}), f32[128,1,128]{2,0,1:T(8,128)}) %reduce-scatter.3.cloned.1.call-update) | async-done | bytes 65552 | tf_op jit(solution)/shard_map/reduce_scatter | solution.py:145
  438.6 1.5 convert_element_type.22
  440.0 137.1 %reduce-scatter.5.cloned.1.call-done = f32[128,1,128]{2,0,1:T(8,128)} async-done(((f32[4096,1,128]{2,0,1:T(8,128)}), f32[128,1,128]{2,0,1:T(8,128)}) %reduce-scatter.5.cloned.1.call-update) | async-done | bytes 65552 | tf_op jit(solution)/shard_map/reduce_scatter | solution.py:146
  577.2 1.5 convert_element_type.23
  (51 shorter events, 10.5 us)
Async XLA Ops:
  7.2 59.4 %all-gather.6.cloned.1.call-start = ((), (), s32[]{:S(2)}) async-start(), calls=%async_computation.3 | async-start | bytes 1310720 | tf_op jit(solution)/shard_map/all_gather | solution.py:106
  8.9 166.8 %all-gather.10.cloned.1.call-start = ((), (), s32[]{:S(2)}) async-start(), calls=%async_computation.7 | async-start | bytes 10485760 | tf_op jit(solution)/shard_map/all_gather | solution.py:12
  103.3 0.8 copy-start.2
  103.3 9.5 %copy-start.1 = (bf16[128,8,128]{2,1,0:T(8,128)(2,1)S(1)}, bf16[128,8,128]{2,1,0:T(8,128)(2,1)}, u32[]{:S(2)}) copy-start(bf16[128,8,128]{2,1,0:T(8,128)(2,1)} %param.11) | copy-start | bytes 786436
  105.3 91.0 %all-to-all-start = ((bf16[32,128,1,128]{3,1,2,0:T(8,128)(2,1)}), bf16[32,128,1,128]{3,1,2,0:T(8,128)(2,1)}, u32[]{:S(2)}, u32[]{:S(2)}) async-start(bf16[32,128,1,128]{3,1,2,0:T(8,128)(2,1)} %stack.2), calls=%async_computation | async-start | bytes 2097152 | tf_op jit(solution)/shard_map/all_to_all | solution.py:136
  112.1 124.1 %all-gather.8.cloned.1.call-start = ((), (), s32[]{:S(2)}) async-start(), calls=%async_computation.4 | async-start | bytes 1081344 | tf_op jit(solution)/shard_map/all_gather | solution.py:139
  112.8 325.8 %reduce-scatter.3.cloned.1.call-start = ((), (), s32[]{:S(2)}) async-start(), calls=%async_computation.5 | async-start | bytes 2162688 | tf_op jit(solution)/shard_map/reduce_scatter | solution.py:145
  192.1 44.0 %copy-start = (bf16[128,8,128]{2,0,1:T(8,128)(2,1)S(1)}, bf16[128,8,128]{2,0,1:T(8,128)(2,1)}, u32[]{:S(2)}) copy-start(bf16[128,8,128]{2,0,1:T(8,128)(2,1)} %copy.52) | copy-start | bytes 786436
  299.2 278.0 %reduce-scatter.5.cloned.1.call-start = ((), (), s32[]{:S(2)}) async-start(), calls=%async_computation.6 | async-start | bytes 2162688 | tf_op jit(solution)/shard_map/reduce_scatter | solution.py:146
Sparse Core Ops, SparseCore 0:
  10.4 27.1 all-gather.5
  103.5 72.1 all-gather.9
  177.6 58.5 all-gather.7
  299.3 139.1 reduce-scatter.2
  440.9 136.1 reduce-scatter.4
